TPU v7x, 256 devices: a whole 4x4x8 slice. The times are simulated.
256 devices in a mesh: shuf: 4 (over y_lo, core), key: 64 (over x, z, y_hi).
Axes of the slice: x: 4, y: 4 (y_hi: 2, y_lo: 2; y = y_hi * 2 + y_lo), z: 8, core: 2. Of those that a mesh axis runs over, the one named last changes fastest.
Arguments:
- embeddings: bfloat16 [32768, 1024], P(('shuf', 'key')), may hold values from -200 to 200
- labels: int32 [32768], P(('shuf', 'key')), may hold values from 0 to 2047
- order: int32 [256, 128], P(('shuf', 'key')), may hold values from 0 to 127, each once within a row
- head_weight: bfloat16 [1024, 512], replicated, may hold values from -0.1875 to 0.1875
Outputs:
- grad_embeddings: bfloat16 [32768, 1024], P(('shuf', 'key'))
- grad_head: float32 [1024, 512], P('key')
All inputs are finite; a program needn't handle non-finite values.
Results may differ from a plain program's by a relative error of at most 0.0075.
Values may be sent and summed in bfloat16 or wider, within the bound.
No kernel may reach another device: no remote copies, remote signals or barrier semaphores. Data moves between devices by JAX's collectives and lax.ppermute only.
A program may use at most 64 MiB of HBM per device.

v0:
```python
import jax
import jax.numpy as jnp
from jax import lax
from jax.sharding import Mesh, PartitionSpec as P

exponent_divisor = 0.1
loss_scale = 64.0
epsilon = 1e-06
AXES = ("yl", "c", "x", "zh", "zl", "yh")
KEY = ("x", "zh", "zl", "yh")
LABEL_ROWS = 16
f32 = jnp.float32
bf16 = jnp.bfloat16


def shift(value, axis, size, distance):
    distance %= size
    if distance == 0:
        return value
    return lax.ppermute(value, axis, [(i, (i + distance) % size) for i in range(size)])


def shift_y(value, distance):
    if distance % 4 == 0:
        return value
    seat = [y % 2 * 2 + y // 2 for y in range(4)]
    return lax.ppermute(
        value, ("yl", "yh"), [(seat[y], seat[(y + distance) % 4]) for y in range(4)]
    )


def unpack(stack, rows):
    normed = stack[:, :rows].reshape(-1, stack.shape[2])
    high = stack[:, rows, :rows].astype(jnp.int32)
    low = stack[:, rows, rows : 2 * rows].astype(jnp.int32)
    return (normed, (high * 64 + low).reshape(-1))


def body(embeddings, labels, order, head_weight):
    rows, width = embeddings.shape
    proj = head_weight.shape[1]
    zh = lax.axis_index("zh")
    share = rows // 4
    doubled = jnp.concatenate([order[0], order[0]])
    routing = lax.dynamic_slice_in_dim(doubled, zh * share, rows)
    with jax.named_scope("route_out"):
        pick = (routing[:, None] == jnp.arange(rows, dtype=jnp.int32)[None, :]).astype(bf16)
        lane = jnp.arange(128, dtype=jnp.int32)[None, :]
        tag = jnp.where(
            lane == 0, (labels // 64)[:, None], jnp.where(lane == 1, (labels % 64)[:, None], 0)
        ).astype(bf16)
        tagged = jnp.concatenate([embeddings, tag], axis=1)
        sent = jnp.dot(pick, tagged, preferred_element_type=f32).astype(bf16)
        sent = sent.reshape(4, share, width + 128)
        got = jnp.concatenate([shift(sent[d], "zh", 4, d) for d in range(4)], axis=0)
    group_rows = got[:, :width]

    def project(values):
        projected = jnp.dot(values, head_weight, preferred_element_type=f32)
        norm = jnp.sqrt(jnp.sum(projected * projected, axis=1, keepdims=True) + epsilon)
        return (projected / norm, norm)

    with jax.named_scope("project"):
        direction, row_norm = project(group_rows)
        normed = direction.astype(bf16)
        label_line = jnp.concatenate(
            [got[:, width], got[:, width + 1], jnp.zeros((proj - 2 * rows,), bf16)]
        )
        label_block = jnp.broadcast_to(label_line[None, :], (LABEL_ROWS, proj))
        packet = jnp.concatenate([normed, label_block], axis=0)
    with jax.named_scope("gather_sets"):
        across_x = jnp.stack([shift(got, "x", 4, d) for d in range(4)])
        across_y = [shift_y(packet, d) for d in range(4)]
        set_b = jnp.stack([shift(block, "zl", 2, dz) for block in across_y for dz in range(2)])
        normed_b, labels_b = unpack(set_b, rows)
        set_a = jnp.concatenate([across_x, shift(across_x, "c", 2, 1)], axis=0)
        set_a = set_a.reshape(-1, width + 128)
        rows_a = set_a[:, :width]
        high = set_a[:, width].astype(jnp.int32)
        labels_a = high * 64 + set_a[:, width + 1].astype(jnp.int32)
        direction_a, norm_a = project(rows_a)
        normed_a = direction_a.astype(bf16)
    with jax.named_scope("scores"):
        total = normed_a.shape[0]
        scores = (
            lax.dot_general(
                normed_a, normed_b, (((1,), (1,)), ((), ())), preferred_element_type=f32
            )
            / exponent_divisor
        )
        row = jnp.arange(total, dtype=jnp.int32)
        itself = jnp.logical_and(row[:, None] == row[None, :], (row < rows)[:, None])
        exponent = jnp.where(itself, 0.0, jnp.exp(scores))
        positive = jnp.logical_and(
            labels_a[:, None] == labels_b[None, :], jnp.logical_not(itself)
        ).astype(f32)
        sums_a = jnp.stack([jnp.sum(exponent, axis=1), jnp.sum(positive, axis=1)])
        sums_b = jnp.stack([jnp.sum(exponent, axis=0), jnp.sum(positive, axis=0)])
    with jax.named_scope("totals"):
        sums_a = sums_a.reshape(2, 2, 4, rows)
        sums_a = sums_a + jnp.roll(shift(sums_a, "c", 2, 1), 1, axis=1)
        sums_a = sum([jnp.roll(shift(sums_a, "x", 4, d), d, axis=2) for d in range(4)])
        sums_b = sums_b.reshape(2, 4, 2, rows)
        sums_b = sums_b + jnp.roll(shift(sums_b, "zl", 2, 1), 1, axis=2)
        sums_b = sum([jnp.roll(shift_y(sums_b, d), d, axis=1) for d in range(4)])

        def weights(sums):
            totals, counts = sums.reshape(2, total)
            floor_count = jnp.maximum(counts, 1.0)
            return (loss_scale * counts / (floor_count * totals), loss_scale / floor_count)

        soft_a, pos_a = weights(sums_a)
        soft_b, pos_b = weights(sums_b)
    with jax.named_scope("pull"):
        half = total // 2

        def pull_rows(start):
            take = slice(start, start + half)
            coefficient = (
                (soft_a[take, None] + soft_b[None, :]) * exponent[take]
                - (pos_a[take, None] + pos_b[None, :]) * positive[take]
            ).astype(bf16)
            part = jnp.dot(coefficient, normed_b, preferred_element_type=f32)
            return part.reshape(4, rows, proj)

        pull_far = pull_rows(half)
        crossing = shift(pull_far, "c", 2, 1)
        pull_near = lax.optimization_barrier(pull_rows(0))

    def to_slopes(pull_grad, unit, norm):
        along = jnp.sum(unit * pull_grad, axis=1, keepdims=True)
        return ((pull_grad - unit * along) / norm).astype(bf16)

    with jax.named_scope("head"):
        pull_part = jnp.concatenate([pull_near, pull_far]).reshape(total, proj)
        slopes_part = to_slopes(pull_part / exponent_divisor, direction_a, norm_a)
        part = lax.dot_general(
            rows_a, slopes_part, (((0,), (0,)), ((), ())), preferred_element_type=f32
        )
        part = part.reshape(64, 2, width // 128, proj)
        core = lax.axis_index("c")
        kept = lax.dynamic_index_in_dim(part, core, axis=1, keepdims=False)
        given = lax.dynamic_index_in_dim(part, 1 - core, axis=1, keepdims=False)
        part = (kept + shift(given.astype(bf16), "c", 2, 1).astype(f32)).astype(bf16)
        spread = lax.all_to_all(part, KEY, split_axis=0, concat_axis=0, tiled=True)
        piece = jnp.sum(spread.astype(f32), axis=0)
        piece = piece + shift(piece, "yl", 2, 1)
        grad_head = lax.all_gather(piece, "c", axis=0, tiled=True)
    with jax.named_scope("slopes"):
        pull = pull_near + crossing
        parts = [shift(pull[d].astype(bf16), "x", 4, -d).astype(f32) for d in range(1, 4)]
        pull_grad = (pull[0] + sum(parts)) / exponent_divisor
        slopes = to_slopes(pull_grad, direction, row_norm)
    with jax.named_scope("route_back"):
        blocks = slopes.reshape(4, share, proj)
        returned = jnp.concatenate([shift(blocks[d], "zh", 4, -d) for d in range(4)], axis=0)
        own = lax.dot_general(
            pick, returned, (((0,), (0,)), ((), ())), preferred_element_type=f32
        ).astype(bf16)
        grad_embeddings = lax.dot_general(
            own, head_weight, (((1,), (1,)), ((), ())), preferred_element_type=f32
        ).astype(bf16)
    return (grad_embeddings, grad_head / loss_scale)


def solution(mesh):
    split = Mesh(mesh.devices.reshape(2, 2, 4, 4, 2, 2), AXES)
    return jax.shard_map(
        body,
        mesh=split,
        in_specs=(P(AXES, None), P(AXES), P(AXES, None), P()),
        out_specs=(P(AXES, None), P(KEY, None)),
        check_vma=False,
    )
```

profile of v0, /device:TPU:1, one launch (start us, length us, event | category | flops | bytes accessed | tf_op | source)
XLA Modules:
  0.0 137.2 jit_solution(9923911454990041922)
XLA Ops:
  3.5 3.9 %collective-permute-start = (bf16[32,1152]{1,0:T(8,128)(2,1)S(1)}, bf16[32,1152]{1,0:T(8,128)(2,1)S(1)}, u32[]{:S(2)}, u32[]{:S(2)}) collective-permute-start(bf16[32,1152]{1,0:T(8,128)(2,1)S(1)} %get-tuple-element.22), channel_id=1, source_target_pairs={{0,4},{4,8},{8,12},{12,0},{1,5},{5,9},{9,13},{13,1},{2,6},{6,10},{... | collective-permute-start | bytes 221192 | tf_op jit(solution)/shard_map/route_out/ppermute | solution.py:20
  7.4 5.1 %collective-permute-start.1 = (bf16[32,1152]{1,0:T(8,128)(2,1)S(1)}, bf16[32,1152]{1,0:T(8,128)(2,1)S(1)}, u32[]{:S(2)}, u32[]{:S(2)}) collective-permute-start(bf16[32,1152]{1,0:T(8,128)(2,1)S(1)} %get-tuple-element.21), channel_id=1, source_target_pairs={{0,8},{4,12},{8,0},{12,4},{1,9},{5,13},{9,1},{13,5},{2,10},{6,14},... | collective-permute-start | bytes 221192 | tf_op jit(solution)/shard_map/route_out/ppermute | solution.py:20
  12.6 2.4 %collective-permute-start.2 = (bf16[32,1152]{1,0:T(8,128)(2,1)S(1)}, bf16[32,1152]{1,0:T(8,128)(2,1)S(1)}, u32[]{:S(2)}, u32[]{:S(2)}) collective-permute-start(bf16[32,1152]{1,0:T(8,128)(2,1)S(1)} %get-tuple-element.20), channel_id=1, source_target_pairs={{0,12},{4,0},{8,4},{12,8},{1,13},{5,1},{9,5},{13,9},{2,14},{6,2},{... | collective-permute-start | bytes 221192 | tf_op jit(solution)/shard_map/route_out/ppermute | solution.py:20
  16.9 3.9 %collective-permute-done.2 = bf16[32,1152]{1,0:T(8,128)(2,1)S(1)} collective-permute-done((bf16[32,1152]{1,0:T(8,128)(2,1)S(1)}, bf16[32,1152]{1,0:T(8,128)(2,1)S(1)}, u32[]{:S(2)}, u32[]{:S(2)}) %collective-permute-start.2) | collective-permute-done | bytes 73760 | tf_op jit(solution)/shard_map/route_out/ppermute | solution.py:20
  22.2 2.5 %collective-permute-start.4 = (bf16[128,1152]{1,0:T(8,128)(2,1)S(1)}, bf16[128,1152]{1,0:T(8,128)(2,1)S(1)}, u32[]{:S(2)}, u32[]{:S(2)}) collective-permute-start(bf16[128,1152]{1,0:T(8,128)(2,1)S(1)} %get-tuple-element.18), channel_id=1, source_target_pairs={{0,32},{16,48},{32,0},{48,16},{1,33},{17,49},{33,1},{49,17},{2,34}... | collective-permute-start | bytes 884744 | tf_op jit(solution)/shard_map/gather_sets/ppermute | solution.py:20
  28.1 2.9 %collective-permute-done.7 = bf16[144,512]{1,0:T(8,128)(2,1)S(1)} collective-permute-done((bf16[144,512]{1,0:T(8,128)(2,1)S(1)}, bf16[144,512]{1,0:T(8,128)(2,1)S(1)}, u32[]{:S(2)}, u32[]{:S(2)}) %collective-permute-start.7) | collective-permute-done | bytes 147488 | tf_op jit(solution)/shard_map/gather_sets/ppermute | solution.py:20
  30.9 2.9 %collective-permute-start.10 = (bf16[144,512]{1,0:T(8,128)(2,1)S(1)}, bf16[144,512]{1,0:T(8,128)(2,1)S(1)}, u32[]{:S(2)}, u32[]{:S(2)}) collective-permute-start(bf16[144,512]{1,0:T(8,128)(2,1)S(1)} %pad_maximum_fusion.2), channel_id=1, source_target_pairs={{0,1},{128,129},{1,0},{129,128},{2,3},{130,131},{3,2},{131,130},{4... | collective-permute-start | bytes 442376 | tf_op jit(solution)/shard_map/gather_sets/ppermute | solution.py:27
  40.7 3.9 %collective-permute-start.6 = (bf16[4,128,1152]{2,1,0:T(8,128)(2,1)S(1)}, bf16[4,128,1152]{2,1,0:T(8,128)(2,1)S(1)}, u32[]{:S(2)}, u32[]{:S(2)}) collective-permute-start(bf16[4,128,1152]{2,1,0:T(8,128)(2,1)S(1)} %pad_maximum_fusion), channel_id=1, source_target_pairs={{0,64},{64,0},{1,65},{65,1},{2,66},{66,2},{3,67},{67,3},{4,68},{68... | collective-permute-start | bytes 3538952 | tf_op jit(solution)/shard_map/gather_sets/ppermute | solution.py:20
  53.1 2.2 %fusion.9 = (f32[1024]{0:T(1024)S(1)}, f32[1024]{0:T(1024)S(1)}) fusion(pred[1024]{0:T(1024)(128)(4,1)S(1)} %iota_compare_fusion.5, s32[1024]{0:T(1024)S(1)} %bitcast.109, s32[1024]{0:T(1024)S(1)} %bitcast.111), kind=kLoop, calls=%fused_computation.20 | loop fusion | flops 8386560 | bytes 17408 | tf_op jit(solution)/shard_map/scores/reduce_sum | solution.py:97
  58.6 3.4 %collective-permute-start.14 = (f32[2,2,4,128]{3,2,1,0:T(4,128)S(1)}, f32[2,2,4,128]{3,2,1,0:T(4,128)S(1)}, u32[]{:S(2)}, u32[]{:S(2)}) collective-permute-start(f32[2,2,4,128]{3,2,1,0:T(4,128)S(1)} %pad_maximum_fusion.3), channel_id=1, source_target_pairs={{0,64},{64,0},{1,65},{65,1},{2,66},{66,2},{3,67},{67,3},{4,68},{68... | collective-permute-start | bytes 24584 | tf_op jit(solution)/shard_map/totals/ppermute | solution.py:20
  67.3 2.3 %collective-permute-start.17 = (f32[2,2,4,128]{3,2,1,0:T(4,128)S(1)}, f32[2,2,4,128]{3,2,1,0:T(4,128)S(1)}, u32[]{:S(2)}, u32[]{:S(2)}) collective-permute-start(f32[2,2,4,128]{3,2,1,0:T(4,128)S(1)} %maximum_add_fusion), channel_id=1, source_target_pairs={{0,48},{16,0},{32,16},{48,32},{1,49},{17,1},{33,17},{49,33},{2,50}... | collective-permute-start | bytes 24584 | tf_op jit(solution)/shard_map/totals/ppermute | solution.py:20
  71.1 2.2 %collective-permute-done.15 = f32[2,2,4,128]{3,2,1,0:T(4,128)S(1)} collective-permute-done((f32[2,2,4,128]{3,2,1,0:T(4,128)S(1)}, f32[2,2,4,128]{3,2,1,0:T(4,128)S(1)}, u32[]{:S(2)}, u32[]{:S(2)}) %collective-permute-start.15) | collective-permute-done | bytes 8224 | tf_op jit(solution)/shard_map/totals/ppermute | solution.py:20
  76.9 5.8 %collective-permute-start.22 = (f32[4,128,512]{2,1,0:T(8,128)}, f32[4,128,512]{2,1,0:T(8,128)}, u32[]{:S(2)}, u32[]{:S(2)}) collective-permute-start(f32[4,128,512]{2,1,0:T(8,128)} %fusion.68), channel_id=1, source_target_pairs={{0,64},{64,0},{1,65},{65,1},{2,66},{66,2},{3,67},{67,3},{4,68},{68... | collective-permute-start | bytes 3145736 | tf_op jit(solution)/shard_map/pull/ppermute | solution.py:20
  82.7 2.8 %maximum_multiply_fusion = f32[8,128,512]{2,1,0:T(8,128)} fusion(f32[4,128,512]{2,1,0:T(8,128)} %fusion.68, f32[4,128,512]{2,1,0:T(8,128)S(1)} %fusion.67), kind=kLoop, calls=%fused_computation.15 | loop fusion | flops 1048576 | bytes 4194304 | tf_op jit(solution)/shard_map/head/div | solution.py:136
  89.7 2.9 %fusion.10 = f32[1024,512]{1,0:T(8,128)S(1)} fusion(bf16[1024,1152]{1,0:T(8,128)(2,1)} %bitcast.94, f32[1024,512]{0,1:T(8,128)S(1)} %copy.10, f32[1024]{0:T(1024)S(1)} %multiply_reduce_fusion, f32[1024]{0:T(1024)S(1)} %add_sqrt_fusion, f32[1024,512]{0,1:T(8,128)S(1)} %copy-done.4), kind=kOutput, calls=%fused_computation.21 | convolution fusion | flops 1076363264 | bytes 8396800 | tf_op jit(solution)/shard_map/head/dot_general | solution.py:137
  96.1 2.2 %fusion.14 = bf16[64,8,512]{2,1,0:T(8,128)(2,1)} fusion(bf16[64,8,512]{2,1,0:T(8,128)(2,1)S(1)} %collective-permute-done.29, f32[64,2,8,512]{3,2,1,0:T(8,128)} %bitcast.86, s32[]{:T(128)S(6)} %select_n.40), kind=kLoop, calls=%fused_computation.29 | loop fusion | flops 786432 | bytes 2097156 | tf_op jit(solution)/shard_map/head/convert_element_type | solution.py:144
  98.3 5.3 %all-to-all-start = ((bf16[64,8,512]{2,1,0:T(8,128)(2,1)}), bf16[64,8,512]{2,1,0:T(8,128)(2,1)S(1)}, u32[]{:S(2)}, u32[]{:S(2)}) async-start(bf16[64,8,512]{2,1,0:T(8,128)(2,1)} %fusion.14), calls=%async_computation | async-start | bytes 1048576 | tf_op jit(solution)/shard_map/head/all_to_all | solution.py:145
  105.2 2.5 %collective-permute-start.23 = (bf16[128,512]{1,0:T(8,128)(2,1)S(1)}, bf16[128,512]{1,0:T(8,128)(2,1)S(1)}, u32[]{:S(2)}, u32[]{:S(2)}) collective-permute-start(bf16[128,512]{1,0:T(8,128)(2,1)S(1)} %get-tuple-element.14), channel_id=1, source_target_pairs={{0,48},{16,0},{32,16},{48,32},{1,49},{17,1},{33,17},{49,33},{2,50}... | collective-permute-start | bytes 393224 | tf_op jit(solution)/shard_map/slopes/ppermute | solution.py:20
  108.7 4.0 %collective-permute-done.23 = bf16[128,512]{1,0:T(8,128)(2,1)S(1)} collective-permute-done((bf16[128,512]{1,0:T(8,128)(2,1)S(1)}, bf16[128,512]{1,0:T(8,128)(2,1)S(1)}, u32[]{:S(2)}, u32[]{:S(2)}) %collective-permute-start.23) | collective-permute-done | bytes 131104 | tf_op jit(solution)/shard_map/slopes/ppermute | solution.py:20
  112.7 3.4 %collective-permute-done.24 = bf16[128,512]{1,0:T(8,128)(2,1)S(1)} collective-permute-done((bf16[128,512]{1,0:T(8,128)(2,1)S(1)}, bf16[128,512]{1,0:T(8,128)(2,1)S(1)}, u32[]{:S(2)}, u32[]{:S(2)}) %collective-permute-start.24) | collective-permute-done | bytes 131104 | tf_op jit(solution)/shard_map/slopes/ppermute | solution.py:20
  116.1 5.6 %collective-permute-done.25 = bf16[128,512]{1,0:T(8,128)(2,1)S(1)} collective-permute-done((bf16[128,512]{1,0:T(8,128)(2,1)S(1)}, bf16[128,512]{1,0:T(8,128)(2,1)S(1)}, u32[]{:S(2)}, u32[]{:S(2)}) %collective-permute-start.25) | collective-permute-done | bytes 131104 | tf_op jit(solution)/shard_map/slopes/ppermute | solution.py:20
  122.0 2.9 %collective-permute-start.26 = (bf16[32,512]{1,0:T(8,128)(2,1)S(1)}, bf16[32,512]{1,0:T(8,128)(2,1)S(1)}, u32[]{:S(2)}, u32[]{:S(2)}) collective-permute-start(bf16[32,512]{1,0:T(8,128)(2,1)S(1)} %get-tuple-element.26), channel_id=1, source_target_pairs={{0,12},{4,0},{8,4},{12,8},{1,13},{5,1},{9,5},{13,9},{2,14},{6,2},{... | collective-permute-start | bytes 98312 | tf_op jit(solution)/shard_map/route_back/ppermute | solution.py:20
  129.2 2.4 %collective-permute-done.27 = bf16[32,512]{1,0:T(8,128)(2,1)S(1)} collective-permute-done((bf16[32,512]{1,0:T(8,128)(2,1)S(1)}, bf16[32,512]{1,0:T(8,128)(2,1)S(1)}, u32[]{:S(2)}, u32[]{:S(2)}) %collective-permute-start.27) | collective-permute-done | bytes 32800 | tf_op jit(solution)/shard_map/route_back/ppermute | solution.py:20
  133.0 3.6 %all_gather.3 = f32[16,512]{1,0:T(8,128)S(1)} all-gather(f32[8,512]{1,0:T(8,128)S(1)} %add.178), channel_id=1, replica_groups=mesh['yl'=2,'c'=2,'x'=4,'zh'=4,'zl'=2,'yh'=2] {'c'}, dimensions={0}, use_global_device_ids=true | all-gather | bytes 49152 | tf_op jit(solution)/shard_map/head/all_gather | solution.py:148
  (138 shorter events, 54.9 us)
Async XLA Ops:
  3.5 11.4 %collective-permute-start = (bf16[32,1152]{1,0:T(8,128)(2,1)S(1)}, bf16[32,1152]{1,0:T(8,128)(2,1)S(1)}, u32[]{:S(2)}, u32[]{:S(2)}) collective-permute-start(bf16[32,1152]{1,0:T(8,128)(2,1)S(1)} %get-tuple-element.22), channel_id=1, source_target_pairs={{0,4},{4,8},{8,12},{12,0},{1,5},{5,9},{9,13},{13,1},{2,6},{6,10},{... | collective-permute-start | bytes 221192 | tf_op jit(solution)/shard_map/route_out/ppermute | solution.py:20
  7.4 9.5 %collective-permute-start.1 = (bf16[32,1152]{1,0:T(8,128)(2,1)S(1)}, bf16[32,1152]{1,0:T(8,128)(2,1)S(1)}, u32[]{:S(2)}, u32[]{:S(2)}) collective-permute-start(bf16[32,1152]{1,0:T(8,128)(2,1)S(1)} %get-tuple-element.21), channel_id=1, source_target_pairs={{0,8},{4,12},{8,0},{12,4},{1,9},{5,13},{9,1},{13,5},{2,10},{6,14},... | collective-permute-start | bytes 221192 | tf_op jit(solution)/shard_map/route_out/ppermute | solution.py:20
  12.6 8.3 %collective-permute-start.2 = (bf16[32,1152]{1,0:T(8,128)(2,1)S(1)}, bf16[32,1152]{1,0:T(8,128)(2,1)S(1)}, u32[]{:S(2)}, u32[]{:S(2)}) collective-permute-start(bf16[32,1152]{1,0:T(8,128)(2,1)S(1)} %get-tuple-element.20), channel_id=1, source_target_pairs={{0,12},{4,0},{8,4},{12,8},{1,13},{5,1},{9,5},{13,9},{2,14},{6,2},{... | collective-permute-start | bytes 221192 | tf_op jit(solution)/shard_map/route_out/ppermute | solution.py:20
  20.9 18.2 %collective-permute-start.3 = (bf16[128,1152]{1,0:T(8,128)(2,1)S(1)}, bf16[128,1152]{1,0:T(8,128)(2,1)S(1)}, u32[]{:S(2)}, u32[]{:S(2)}) collective-permute-start(bf16[128,1152]{1,0:T(8,128)(2,1)S(1)} %get-tuple-element.18), channel_id=1, source_target_pairs={{0,16},{16,32},{32,48},{48,0},{1,17},{17,33},{33,49},{49,1},{2,18}... | collective-permute-start | bytes 884744 | tf_op jit(solution)/shard_map/gather_sets/ppermute | solution.py:20
  22.2 18.4 %collective-permute-start.4 = (bf16[128,1152]{1,0:T(8,128)(2,1)S(1)}, bf16[128,1152]{1,0:T(8,128)(2,1)S(1)}, u32[]{:S(2)}, u32[]{:S(2)}) collective-permute-start(bf16[128,1152]{1,0:T(8,128)(2,1)S(1)} %get-tuple-element.18), channel_id=1, source_target_pairs={{0,32},{16,48},{32,0},{48,16},{1,33},{17,49},{33,1},{49,17},{2,34}... | collective-permute-start | bytes 884744 | tf_op jit(solution)/shard_map/gather_sets/ppermute | solution.py:20
  24.6 15.9 %collective-permute-start.5 = (bf16[128,1152]{1,0:T(8,128)(2,1)S(1)}, bf16[128,1152]{1,0:T(8,128)(2,1)S(1)}, u32[]{:S(2)}, u32[]{:S(2)}) collective-permute-start(bf16[128,1152]{1,0:T(8,128)(2,1)S(1)} %get-tuple-element.18), channel_id=1, source_target_pairs={{0,48},{16,0},{32,16},{48,32},{1,49},{17,1},{33,17},{49,33},{2,50}... | collective-permute-start | bytes 884744 | tf_op jit(solution)/shard_map/gather_sets/ppermute | solution.py:20
  26.6 7.2 %collective-permute-start.8 = (bf16[144,512]{1,0:T(8,128)(2,1)S(1)}, bf16[144,512]{1,0:T(8,128)(2,1)S(1)}, u32[]{:S(2)}, u32[]{:S(2)}) collective-permute-start(bf16[144,512]{1,0:T(8,128)(2,1)S(1)} %pad_maximum_fusion.2), channel_id=1, source_target_pairs={{0,128},{128,1},{1,129},{129,0},{2,130},{130,3},{3,131},{131,2},{4... | collective-permute-start | bytes 442376 | tf_op jit(solution)/shard_map/gather_sets/ppermute | solution.py:27
  30.9 5.9 %collective-permute-start.10 = (bf16[144,512]{1,0:T(8,128)(2,1)S(1)}, bf16[144,512]{1,0:T(8,128)(2,1)S(1)}, u32[]{:S(2)}, u32[]{:S(2)}) collective-permute-start(bf16[144,512]{1,0:T(8,128)(2,1)S(1)} %pad_maximum_fusion.2), channel_id=1, source_target_pairs={{0,1},{128,129},{1,0},{129,128},{2,3},{130,131},{3,2},{131,130},{4... | collective-permute-start | bytes 442376 | tf_op jit(solution)/shard_map/gather_sets/ppermute | solution.py:27
  33.9 5.2 %collective-permute-start.12 = (bf16[144,512]{1,0:T(8,128)(2,1)S(1)}, bf16[144,512]{1,0:T(8,128)(2,1)S(1)}, u32[]{:S(2)}, u32[]{:S(2)}) collective-permute-start(bf16[144,512]{1,0:T(8,128)(2,1)S(1)} %pad_maximum_fusion.2), channel_id=1, source_target_pairs={{0,129},{128,0},{1,128},{129,1},{2,131},{130,2},{3,130},{131,3},{4... | collective-permute-start | bytes 442376 | tf_op jit(solution)/shard_map/gather_sets/ppermute | solution.py:27
  36.8 7.9 %collective-permute-start.9 = (bf16[144,512]{1,0:T(8,128)(2,1)S(1)}, bf16[144,512]{1,0:T(8,128)(2,1)S(1)}, u32[]{:S(2)}, u32[]{:S(2)}) collective-permute-start(bf16[144,512]{1,0:T(8,128)(2,1)S(1)} %collective-permute-done.8), channel_id=1, source_target_pairs={{0,2},{2,0},{1,3},{3,1},{4,6},{6,4},{5,7},{7,5},{8,10},{10,8},{9,1... | collective-permute-start | bytes 442376 | tf_op jit(solution)/shard_map/gather_sets/ppermute | solution.py:20
  39.1 5.7 %collective-permute-start.11 = (bf16[144,512]{1,0:T(8,128)(2,1)S(1)}, bf16[144,512]{1,0:T(8,128)(2,1)S(1)}, u32[]{:S(2)}, u32[]{:S(2)}) collective-permute-start(bf16[144,512]{1,0:T(8,128)(2,1)S(1)} %collective-permute-done.10), channel_id=1, source_target_pairs={{0,2},{2,0},{1,3},{3,1},{4,6},{6,4},{5,7},{7,5},{8,10},{10,8},{9,1... | collective-permute-start | bytes 442376 | tf_op jit(solution)/shard_map/gather_sets/ppermute | solution.py:20
  39.1 7.9 %collective-permute-start.13 = (bf16[144,512]{1,0:T(8,128)(2,1)S(1)}, bf16[144,512]{1,0:T(8,128)(2,1)S(1)}, u32[]{:S(2)}, u32[]{:S(2)}) collective-permute-start(bf16[144,512]{1,0:T(8,128)(2,1)S(1)} %collective-permute-done.12), channel_id=1, source_target_pairs={{0,2},{2,0},{1,3},{3,1},{4,6},{6,4},{5,7},{7,5},{8,10},{10,8},{9,1... | collective-permute-start | bytes 442376 | tf_op jit(solution)/shard_map/gather_sets/ppermute | solution.py:20
  40.7 7.4 %collective-permute-start.6 = (bf16[4,128,1152]{2,1,0:T(8,128)(2,1)S(1)}, bf16[4,128,1152]{2,1,0:T(8,128)(2,1)S(1)}, u32[]{:S(2)}, u32[]{:S(2)}) collective-permute-start(bf16[4,128,1152]{2,1,0:T(8,128)(2,1)S(1)} %pad_maximum_fusion), channel_id=1, source_target_pairs={{0,64},{64,0},{1,65},{65,1},{2,66},{66,2},{3,67},{67,3},{4,68},{68... | collective-permute-start | bytes 3538952 | tf_op jit(solution)/shard_map/gather_sets/ppermute | solution.py:20
  58.6 8.3 %collective-permute-start.14 = (f32[2,2,4,128]{3,2,1,0:T(4,128)S(1)}, f32[2,2,4,128]{3,2,1,0:T(4,128)S(1)}, u32[]{:S(2)}, u32[]{:S(2)}) collective-permute-start(f32[2,2,4,128]{3,2,1,0:T(4,128)S(1)} %pad_maximum_fusion.3), channel_id=1, source_target_pairs={{0,64},{64,0},{1,65},{65,1},{2,66},{66,2},{3,67},{67,3},{4,68},{68... | collective-permute-start | bytes 24584 | tf_op jit(solution)/shard_map/totals/ppermute | solution.py:20
  62.1 7.6 %collective-permute-start.20 = (f32[2,4,2,128]{3,2,1,0:T(2,128)S(1)}, f32[2,4,2,128]{3,2,1,0:T(2,128)S(1)}, u32[]{:S(2)}, u32[]{:S(2)}) collective-permute-start(f32[2,4,2,128]{3,2,1,0:T(2,128)S(1)} %maximum_add_fusion.2), channel_id=1, source_target_pairs={{0,1},{128,129},{1,0},{129,128},{2,3},{130,131},{3,2},{131,130},{4... | collective-permute-start | bytes 24584 | tf_op jit(solution)/shard_map/totals/ppermute | solution.py:27
  64.3 5.4 %collective-permute-start.19 = (f32[2,4,2,128]{3,2,1,0:T(2,128)S(1)}, f32[2,4,2,128]{3,2,1,0:T(2,128)S(1)}, u32[]{:S(2)}, u32[]{:S(2)}) collective-permute-start(f32[2,4,2,128]{3,2,1,0:T(2,128)S(1)} %maximum_add_fusion.2), channel_id=1, source_target_pairs={{0,128},{128,1},{1,129},{129,0},{2,130},{130,3},{3,131},{131,2},{4... | collective-permute-start | bytes 24584 | tf_op jit(solution)/shard_map/totals/ppermute | solution.py:27
  76.9 26.7 %collective-permute-start.22 = (f32[4,128,512]{2,1,0:T(8,128)}, f32[4,128,512]{2,1,0:T(8,128)}, u32[]{:S(2)}, u32[]{:S(2)}) collective-permute-start(f32[4,128,512]{2,1,0:T(8,128)} %fusion.68), channel_id=1, source_target_pairs={{0,64},{64,0},{1,65},{65,1},{2,66},{66,2},{3,67},{67,3},{4,68},{68... | collective-permute-start | bytes 3145736 | tf_op jit(solution)/shard_map/pull/ppermute | solution.py:20
  98.3 30.0 %all-to-all-start = ((bf16[64,8,512]{2,1,0:T(8,128)(2,1)}), bf16[64,8,512]{2,1,0:T(8,128)(2,1)S(1)}, u32[]{:S(2)}, u32[]{:S(2)}) async-start(bf16[64,8,512]{2,1,0:T(8,128)(2,1)} %fusion.14), calls=%async_computation | async-start | bytes 1048576 | tf_op jit(solution)/shard_map/head/all_to_all | solution.py:145
  105.2 7.5 %collective-permute-start.23 = (bf16[128,512]{1,0:T(8,128)(2,1)S(1)}, bf16[128,512]{1,0:T(8,128)(2,1)S(1)}, u32[]{:S(2)}, u32[]{:S(2)}) collective-permute-start(bf16[128,512]{1,0:T(8,128)(2,1)S(1)} %get-tuple-element.14), channel_id=1, source_target_pairs={{0,48},{16,0},{32,16},{48,32},{1,49},{17,1},{33,17},{49,33},{2,50}... | collective-permute-start | bytes 393224 | tf_op jit(solution)/shard_map/slopes/ppermute | solution.py:20
  107.7 8.4 %collective-permute-start.24 = (bf16[128,512]{1,0:T(8,128)(2,1)S(1)}, bf16[128,512]{1,0:T(8,128)(2,1)S(1)}, u32[]{:S(2)}, u32[]{:S(2)}) collective-permute-start(bf16[128,512]{1,0:T(8,128)(2,1)S(1)} %get-tuple-element.16), channel_id=1, source_target_pairs={{0,32},{16,48},{32,0},{48,16},{1,33},{17,49},{33,1},{49,17},{2,34}... | collective-permute-start | bytes 393224 | tf_op jit(solution)/shard_map/slopes/ppermute | solution.py:20
  108.1 13.6 %collective-permute-start.25 = (bf16[128,512]{1,0:T(8,128)(2,1)S(1)}, bf16[128,512]{1,0:T(8,128)(2,1)S(1)}, u32[]{:S(2)}, u32[]{:S(2)}) collective-permute-start(bf16[128,512]{1,0:T(8,128)(2,1)S(1)} %get-tuple-element.15), channel_id=1, source_target_pairs={{0,16},{16,32},{32,48},{48,0},{1,17},{17,33},{33,49},{49,1},{2,18}... | collective-permute-start | bytes 393224 | tf_op jit(solution)/shard_map/slopes/ppermute | solution.py:20
  122.0 7.2 %collective-permute-start.26 = (bf16[32,512]{1,0:T(8,128)(2,1)S(1)}, bf16[32,512]{1,0:T(8,128)(2,1)S(1)}, u32[]{:S(2)}, u32[]{:S(2)}) collective-permute-start(bf16[32,512]{1,0:T(8,128)(2,1)S(1)} %get-tuple-element.26), channel_id=1, source_target_pairs={{0,12},{4,0},{8,4},{12,8},{1,13},{5,1},{9,5},{13,9},{2,14},{6,2},{... | collective-permute-start | bytes 98312 | tf_op jit(solution)/shard_map/route_back/ppermute | solution.py:20
  124.9 6.8 %collective-permute-start.27 = (bf16[32,512]{1,0:T(8,128)(2,1)S(1)}, bf16[32,512]{1,0:T(8,128)(2,1)S(1)}, u32[]{:S(2)}, u32[]{:S(2)}) collective-permute-start(bf16[32,512]{1,0:T(8,128)(2,1)S(1)} %get-tuple-element.25), channel_id=1, source_target_pairs={{0,8},{4,12},{8,0},{12,4},{1,9},{5,13},{9,1},{13,5},{2,10},{6,14},... | collective-permute-start | bytes 98312 | tf_op jit(solution)/shard_map/route_back/ppermute | solution.py:20
  126.4 5.3 %collective-permute-start.28 = (bf16[32,512]{1,0:T(8,128)(2,1)S(1)}, bf16[32,512]{1,0:T(8,128)(2,1)S(1)}, u32[]{:S(2)}, u32[]{:S(2)}) collective-permute-start(bf16[32,512]{1,0:T(8,128)(2,1)S(1)} %get-tuple-element.24), channel_id=1, source_target_pairs={{0,4},{4,8},{8,12},{12,0},{1,5},{5,9},{9,13},{13,1},{2,6},{6,10},{... | collective-permute-start | bytes 98312 | tf_op jit(solution)/shard_map/route_back/ppermute | solution.py:20
  (16 other events, 86.9 us)
where the time goes:
time: 138 us; the launch traced here: 137 us
  starting transfers between devices  60.9 us (44%)
  waiting for transfers between devices  35.1 us (25%)
  other arithmetic  15.6 us (11%)
  matrix products  11.6 us (8%)
  local copies, waits for them, and re-layouts  9.25 us (7%)
  blocking collectives  3.59 us (3%)
    ppermute x25, starting transfers between devices, shift(): lax.ppermute(value, axis, [(i, (i + distance) % size) for i in range(size)])  45.5 us
    ppermute x25, waiting for transfers between devices, shift(): lax.ppermute(value, axis, [(i, (i + distance) % size) for i in range(size)])  31.4 us
    ppermute x6, starting transfers between devices, shift_y(): lax.ppermute(value, ('yl', 'yh'), [(seat[y], seat[(y + distance) % 4]) fo...  10 us
    all_to_all x1, starting transfers between devices, body(): spread = lax.all_to_all(part, KEY, split_axis=0, concat_axis=0, tiled=True)  5.33 us
    unnamed x27, local copies, waits for them, and re-layouts  4.58 us
    ppermute x6, waiting for transfers between devices, shift_y(): lax.ppermute(value, ('yl', 'yh'), [(seat[y], seat[(y + distance) % 4]) fo...  3.67 us
    all_gather x1, blocking collectives, body(): grad_head = lax.all_gather(piece, 'c', axis=0, tiled=True)  3.59 us
    dot_general x1, matrix products, body(): lax.dot_general(rows_a, slopes_part, (((0,), (0,)), ((), ())), preferred_...  2.93 us
  transfers between devices with their start and end apart: 32, of which 13 were waited for; matrix products, arithmetic and copies ran while one was open for 13% of the time, Pallas kernels for 0%

commit v1 on v0

--- a/solution.py
+++ b/solution.py
@@ -145,7 +145,10 @@
         spread = lax.all_to_all(part, KEY, split_axis=0, concat_axis=0, tiled=True)
         piece = jnp.sum(spread.astype(f32), axis=0)
         piece = piece + shift(piece, "yl", 2, 1)
-        grad_head = lax.all_gather(piece, "c", axis=0, tiled=True)
+        count = lax.axis_size("c")
+        pieces = jnp.stack([piece for _ in range(count)])
+        pieces = lax.all_to_all(pieces, "c", split_axis=0, concat_axis=0)
+        grad_head = jnp.concatenate(pieces, axis=0)
     with jax.named_scope("slopes"):
         pull = pull_near + crossing
         parts = [shift(pull[d].astype(bf16), "x", 4, -d).astype(f32) for d in range(1, 4)]

time: 138 us -> 140 us (1.014)
  blocking collectives: 3.59 us -> 5.51 us
    all_to_all x0 -> x1, blocking collectives: none -> 5.51 us  [body(): pieces = lax.all_to_all(pieces, 'c', split_axis=0, concat_axis=0)]
    all_gather x1 -> x0, blocking collectives: 3.59 us -> none  [body(): grad_head = lax.all_gather(piece, 'c', axis=0, tiled=True)]
where the time goes in v1:
time: 140 us; the launch traced here: 139 us
  starting transfers between devices  60.9 us (44%)
  waiting for transfers between devices  35.1 us (25%)
  other arithmetic  15.6 us (11%)
  matrix products  11.6 us (8%)
  local copies, waits for them, and re-layouts  9.25 us (7%)
  blocking collectives  5.51 us (4%)
    ppermute x25, starting transfers between devices, shift(): lax.ppermute(value, axis, [(i, (i + distance) % size) for i in range(size)])  45.5 us
    ppermute x25, waiting for transfers between devices, shift(): lax.ppermute(value, axis, [(i, (i + distance) % size) for i in range(size)])  31.4 us
    ppermute x6, starting transfers between devices, shift_y(): lax.ppermute(value, ('yl', 'yh'), [(seat[y], seat[(y + distance) % 4]) fo...  10 us
    all_to_all x1, blocking collectives, body(): pieces = lax.all_to_all(pieces, 'c', split_axis=0, concat_axis=0)  5.51 us
    all_to_all x1, starting transfers between devices, body(): spread = lax.all_to_all(part, KEY, split_axis=0, concat_axis=0, tiled=True)  5.33 us
    unnamed x27, local copies, waits for them, and re-layouts  4.58 us
    ppermute x6, waiting for transfers between devices, shift_y(): lax.ppermute(value, ('yl', 'yh'), [(seat[y], seat[(y + distance) % 4]) fo...  3.67 us
    dot_general x1, matrix products, body(): lax.dot_general(rows_a, slopes_part, (((0,), (0,)), ((), ())), preferred_...  2.93 us
  transfers between devices with their start and end apart: 32, of which 13 were waited for; matrix products, arithmetic and copies ran while one was open for 13% of the time, Pallas kernels for 0%

profile of v1, /device:TPU:1, one launch (start us, length us, event | category | flops | bytes accessed | tf_op | source)
XLA Modules:
  0.0 139.2 jit_solution(8948073103308956055)
XLA Ops:
  3.5 3.9 %collective-permute-start = (bf16[32,1152]{1,0:T(8,128)(2,1)S(1)}, bf16[32,1152]{1,0:T(8,128)(2,1)S(1)}, u32[]{:S(2)}, u32[]{:S(2)}) collective-permute-start(bf16[32,1152]{1,0:T(8,128)(2,1)S(1)} %get-tuple-element.22), channel_id=1, source_target_pairs={{0,4},{4,8},{8,12},{12,0},{1,5},{5,9},{9,13},{13,1},{2,6},{6,10},{... | collective-permute-start | bytes 221192 | tf_op jit(solution)/shard_map/route_out/ppermute | solution.py:20
  7.4 5.1 %collective-permute-start.1 = (bf16[32,1152]{1,0:T(8,128)(2,1)S(1)}, bf16[32,1152]{1,0:T(8,128)(2,1)S(1)}, u32[]{:S(2)}, u32[]{:S(2)}) collective-permute-start(bf16[32,1152]{1,0:T(8,128)(2,1)S(1)} %get-tuple-element.21), channel_id=1, source_target_pairs={{0,8},{4,12},{8,0},{12,4},{1,9},{5,13},{9,1},{13,5},{2,10},{6,14},... | collective-permute-start | bytes 221192 | tf_op jit(solution)/shard_map/route_out/ppermute | solution.py:20
  12.6 2.4 %collective-permute-start.2 = (bf16[32,1152]{1,0:T(8,128)(2,1)S(1)}, bf16[32,1152]{1,0:T(8,128)(2,1)S(1)}, u32[]{:S(2)}, u32[]{:S(2)}) collective-permute-start(bf16[32,1152]{1,0:T(8,128)(2,1)S(1)} %get-tuple-element.20), channel_id=1, source_target_pairs={{0,12},{4,0},{8,4},{12,8},{1,13},{5,1},{9,5},{13,9},{2,14},{6,2},{... | collective-permute-start | bytes 221192 | tf_op jit(solution)/shard_map/route_out/ppermute | solution.py:20
  16.9 3.9 %collective-permute-done.2 = bf16[32,1152]{1,0:T(8,128)(2,1)S(1)} collective-permute-done((bf16[32,1152]{1,0:T(8,128)(2,1)S(1)}, bf16[32,1152]{1,0:T(8,128)(2,1)S(1)}, u32[]{:S(2)}, u32[]{:S(2)}) %collective-permute-start.2) | collective-permute-done | bytes 73760 | tf_op jit(solution)/shard_map/route_out/ppermute | solution.py:20
  22.2 2.5 %collective-permute-start.4 = (bf16[128,1152]{1,0:T(8,128)(2,1)S(1)}, bf16[128,1152]{1,0:T(8,128)(2,1)S(1)}, u32[]{:S(2)}, u32[]{:S(2)}) collective-permute-start(bf16[128,1152]{1,0:T(8,128)(2,1)S(1)} %get-tuple-element.18), channel_id=1, source_target_pairs={{0,32},{16,48},{32,0},{48,16},{1,33},{17,49},{33,1},{49,17},{2,34}... | collective-permute-start | bytes 884744 | tf_op jit(solution)/shard_map/gather_sets/ppermute | solution.py:20
  28.1 2.9 %collective-permute-done.7 = bf16[144,512]{1,0:T(8,128)(2,1)S(1)} collective-permute-done((bf16[144,512]{1,0:T(8,128)(2,1)S(1)}, bf16[144,512]{1,0:T(8,128)(2,1)S(1)}, u32[]{:S(2)}, u32[]{:S(2)}) %collective-permute-start.7) | collective-permute-done | bytes 147488 | tf_op jit(solution)/shard_map/gather_sets/ppermute | solution.py:20
  30.9 2.9 %collective-permute-start.10 = (bf16[144,512]{1,0:T(8,128)(2,1)S(1)}, bf16[144,512]{1,0:T(8,128)(2,1)S(1)}, u32[]{:S(2)}, u32[]{:S(2)}) collective-permute-start(bf16[144,512]{1,0:T(8,128)(2,1)S(1)} %pad_maximum_fusion.2), channel_id=1, source_target_pairs={{0,1},{128,129},{1,0},{129,128},{2,3},{130,131},{3,2},{131,130},{4... | collective-permute-start | bytes 442376 | tf_op jit(solution)/shard_map/gather_sets/ppermute | solution.py:27
  40.7 3.9 %collective-permute-start.6 = (bf16[4,128,1152]{2,1,0:T(8,128)(2,1)S(1)}, bf16[4,128,1152]{2,1,0:T(8,128)(2,1)S(1)}, u32[]{:S(2)}, u32[]{:S(2)}) collective-permute-start(bf16[4,128,1152]{2,1,0:T(8,128)(2,1)S(1)} %pad_maximum_fusion), channel_id=1, source_target_pairs={{0,64},{64,0},{1,65},{65,1},{2,66},{66,2},{3,67},{67,3},{4,68},{68... | collective-permute-start | bytes 3538952 | tf_op jit(solution)/shard_map/gather_sets/ppermute | solution.py:20
  53.1 2.2 %fusion.9 = (f32[1024]{0:T(1024)S(1)}, f32[1024]{0:T(1024)S(1)}) fusion(pred[1024]{0:T(1024)(128)(4,1)S(1)} %iota_compare_fusion.5, s32[1024]{0:T(1024)S(1)} %bitcast.113, s32[1024]{0:T(1024)S(1)} %bitcast.115), kind=kLoop, calls=%fused_computation.20 | loop fusion | flops 8386560 | bytes 17408 | tf_op jit(solution)/shard_map/scores/reduce_sum | solution.py:97
  58.6 3.4 %collective-permute-start.14 = (f32[2,2,4,128]{3,2,1,0:T(4,128)S(1)}, f32[2,2,4,128]{3,2,1,0:T(4,128)S(1)}, u32[]{:S(2)}, u32[]{:S(2)}) collective-permute-start(f32[2,2,4,128]{3,2,1,0:T(4,128)S(1)} %pad_maximum_fusion.4), channel_id=1, source_target_pairs={{0,64},{64,0},{1,65},{65,1},{2,66},{66,2},{3,67},{67,3},{4,68},{68... | collective-permute-start | bytes 24584 | tf_op jit(solution)/shard_map/totals/ppermute | solution.py:20
  67.3 2.3 %collective-permute-start.17 = (f32[2,2,4,128]{3,2,1,0:T(4,128)S(1)}, f32[2,2,4,128]{3,2,1,0:T(4,128)S(1)}, u32[]{:S(2)}, u32[]{:S(2)}) collective-permute-start(f32[2,2,4,128]{3,2,1,0:T(4,128)S(1)} %maximum_add_fusion), channel_id=1, source_target_pairs={{0,48},{16,0},{32,16},{48,32},{1,49},{17,1},{33,17},{49,33},{2,50}... | collective-permute-start | bytes 24584 | tf_op jit(solution)/shard_map/totals/ppermute | solution.py:20
  71.1 2.2 %collective-permute-done.15 = f32[2,2,4,128]{3,2,1,0:T(4,128)S(1)} collective-permute-done((f32[2,2,4,128]{3,2,1,0:T(4,128)S(1)}, f32[2,2,4,128]{3,2,1,0:T(4,128)S(1)}, u32[]{:S(2)}, u32[]{:S(2)}) %collective-permute-start.15) | collective-permute-done | bytes 8224 | tf_op jit(solution)/shard_map/totals/ppermute | solution.py:20
  76.9 5.8 %collective-permute-start.22 = (f32[4,128,512]{2,1,0:T(8,128)}, f32[4,128,512]{2,1,0:T(8,128)}, u32[]{:S(2)}, u32[]{:S(2)}) collective-permute-start(f32[4,128,512]{2,1,0:T(8,128)} %fusion.68), channel_id=1, source_target_pairs={{0,64},{64,0},{1,65},{65,1},{2,66},{66,2},{3,67},{67,3},{4,68},{68... | collective-permute-start | bytes 3145736 | tf_op jit(solution)/shard_map/pull/ppermute | solution.py:20
  82.7 2.8 %maximum_multiply_fusion = f32[8,128,512]{2,1,0:T(8,128)} fusion(f32[4,128,512]{2,1,0:T(8,128)} %fusion.68, f32[4,128,512]{2,1,0:T(8,128)S(1)} %fusion.67), kind=kLoop, calls=%fused_computation.15 | loop fusion | flops 1048576 | bytes 4194304 | tf_op jit(solution)/shard_map/head/div | solution.py:136
  89.7 2.9 %fusion.10 = f32[1024,512]{1,0:T(8,128)S(1)} fusion(bf16[1024,1152]{1,0:T(8,128)(2,1)} %bitcast.98, f32[1024,512]{0,1:T(8,128)S(1)} %copy.10, f32[1024]{0:T(1024)S(1)} %multiply_reduce_fusion, f32[1024]{0:T(1024)S(1)} %add_sqrt_fusion, f32[1024,512]{0,1:T(8,128)S(1)} %copy-done.4), kind=kOutput, calls=%fused_computation.21 | convolution fusion | flops 1076363264 | bytes 8396800 | tf_op jit(solution)/shard_map/head/dot_general | solution.py:137
  96.1 2.2 %fusion.14 = bf16[64,8,512]{2,1,0:T(8,128)(2,1)} fusion(bf16[64,8,512]{2,1,0:T(8,128)(2,1)S(1)} %collective-permute-done.29, f32[64,2,8,512]{3,2,1,0:T(8,128)} %bitcast.90, s32[]{:T(128)S(6)} %select_n.40), kind=kLoop, calls=%fused_computation.29 | loop fusion | flops 786432 | bytes 2097156 | tf_op jit(solution)/shard_map/head/convert_element_type | solution.py:144
  98.3 5.3 %all-to-all-start = ((bf16[64,8,512]{2,1,0:T(8,128)(2,1)}), bf16[64,8,512]{2,1,0:T(8,128)(2,1)S(1)}, u32[]{:S(2)}, u32[]{:S(2)}) async-start(bf16[64,8,512]{2,1,0:T(8,128)(2,1)} %fusion.14), calls=%async_computation | async-start | bytes 1048576 | tf_op jit(solution)/shard_map/head/all_to_all | solution.py:145
  105.2 2.5 %collective-permute-start.23 = (bf16[128,512]{1,0:T(8,128)(2,1)S(1)}, bf16[128,512]{1,0:T(8,128)(2,1)S(1)}, u32[]{:S(2)}, u32[]{:S(2)}) collective-permute-start(bf16[128,512]{1,0:T(8,128)(2,1)S(1)} %get-tuple-element.14), channel_id=1, source_target_pairs={{0,48},{16,0},{32,16},{48,32},{1,49},{17,1},{33,17},{49,33},{2,50}... | collective-permute-start | bytes 393224 | tf_op jit(solution)/shard_map/slopes/ppermute | solution.py:20
  108.7 4.0 %collective-permute-done.23 = bf16[128,512]{1,0:T(8,128)(2,1)S(1)} collective-permute-done((bf16[128,512]{1,0:T(8,128)(2,1)S(1)}, bf16[128,512]{1,0:T(8,128)(2,1)S(1)}, u32[]{:S(2)}, u32[]{:S(2)}) %collective-permute-start.23) | collective-permute-done | bytes 131104 | tf_op jit(solution)/shard_map/slopes/ppermute | solution.py:20
  112.7 3.4 %collective-permute-done.24 = bf16[128,512]{1,0:T(8,128)(2,1)S(1)} collective-permute-done((bf16[128,512]{1,0:T(8,128)(2,1)S(1)}, bf16[128,512]{1,0:T(8,128)(2,1)S(1)}, u32[]{:S(2)}, u32[]{:S(2)}) %collective-permute-start.24) | collective-permute-done | bytes 131104 | tf_op jit(solution)/shard_map/slopes/ppermute | solution.py:20
  116.1 5.6 %collective-permute-done.25 = bf16[128,512]{1,0:T(8,128)(2,1)S(1)} collective-permute-done((bf16[128,512]{1,0:T(8,128)(2,1)S(1)}, bf16[128,512]{1,0:T(8,128)(2,1)S(1)}, u32[]{:S(2)}, u32[]{:S(2)}) %collective-permute-start.25) | collective-permute-done | bytes 131104 | tf_op jit(solution)/shard_map/slopes/ppermute | solution.py:20
  122.0 2.9 %collective-permute-start.26 = (bf16[32,512]{1,0:T(8,128)(2,1)S(1)}, bf16[32,512]{1,0:T(8,128)(2,1)S(1)}, u32[]{:S(2)}, u32[]{:S(2)}) collective-permute-start(bf16[32,512]{1,0:T(8,128)(2,1)S(1)} %get-tuple-element.26), channel_id=1, source_target_pairs={{0,12},{4,0},{8,4},{12,8},{1,13},{5,1},{9,5},{13,9},{2,14},{6,2},{... | collective-permute-start | bytes 98312 | tf_op jit(solution)/shard_map/route_back/ppermute | solution.py:20
  129.2 2.4 %collective-permute-done.27 = bf16[32,512]{1,0:T(8,128)(2,1)S(1)} collective-permute-done((bf16[32,512]{1,0:T(8,128)(2,1)S(1)}, bf16[32,512]{1,0:T(8,128)(2,1)S(1)}, u32[]{:S(2)}, u32[]{:S(2)}) %collective-permute-start.27) | collective-permute-done | bytes 32800 | tf_op jit(solution)/shard_map/route_back/ppermute | solution.py:20
  133.0 5.5 %all_to_all.10 = f32[2,8,512]{2,1,0:T(8,128)S(1)} all-to-all(f32[2,8,512]{2,1,0:T(8,128)S(1)} %pad_maximum_fusion.3), channel_id=1, replica_groups=mesh['yl'=2,'c'=2,'x'=4,'zh'=4,'zl'=2,'yh'=2] {'c'}, dimensions={0} | all-to-all | bytes 65536 | tf_op jit(solution)/shard_map/head/all_to_all | solution.py:150
  (139 shorter events, 54.9 us)
Async XLA Ops:
  3.5 11.4 %collective-permute-start = (bf16[32,1152]{1,0:T(8,128)(2,1)S(1)}, bf16[32,1152]{1,0:T(8,128)(2,1)S(1)}, u32[]{:S(2)}, u32[]{:S(2)}) collective-permute-start(bf16[32,1152]{1,0:T(8,128)(2,1)S(1)} %get-tuple-element.22), channel_id=1, source_target_pairs={{0,4},{4,8},{8,12},{12,0},{1,5},{5,9},{9,13},{13,1},{2,6},{6,10},{... | collective-permute-start | bytes 221192 | tf_op jit(solution)/shard_map/route_out/ppermute | solution.py:20
  7.4 9.5 %collective-permute-start.1 = (bf16[32,1152]{1,0:T(8,128)(2,1)S(1)}, bf16[32,1152]{1,0:T(8,128)(2,1)S(1)}, u32[]{:S(2)}, u32[]{:S(2)}) collective-permute-start(bf16[32,1152]{1,0:T(8,128)(2,1)S(1)} %get-tuple-element.21), channel_id=1, source_target_pairs={{0,8},{4,12},{8,0},{12,4},{1,9},{5,13},{9,1},{13,5},{2,10},{6,14},... | collective-permute-start | bytes 221192 | tf_op jit(solution)/shard_map/route_out/ppermute | solution.py:20
  12.6 8.3 %collective-permute-start.2 = (bf16[32,1152]{1,0:T(8,128)(2,1)S(1)}, bf16[32,1152]{1,0:T(8,128)(2,1)S(1)}, u32[]{:S(2)}, u32[]{:S(2)}) collective-permute-start(bf16[32,1152]{1,0:T(8,128)(2,1)S(1)} %get-tuple-element.20), channel_id=1, source_target_pairs={{0,12},{4,0},{8,4},{12,8},{1,13},{5,1},{9,5},{13,9},{2,14},{6,2},{... | collective-permute-start | bytes 221192 | tf_op jit(solution)/shard_map/route_out/ppermute | solution.py:20
  20.9 18.2 %collective-permute-start.3 = (bf16[128,1152]{1,0:T(8,128)(2,1)S(1)}, bf16[128,1152]{1,0:T(8,128)(2,1)S(1)}, u32[]{:S(2)}, u32[]{:S(2)}) collective-permute-start(bf16[128,1152]{1,0:T(8,128)(2,1)S(1)} %get-tuple-element.18), channel_id=1, source_target_pairs={{0,16},{16,32},{32,48},{48,0},{1,17},{17,33},{33,49},{49,1},{2,18}... | collective-permute-start | bytes 884744 | tf_op jit(solution)/shard_map/gather_sets/ppermute | solution.py:20
  22.2 18.4 %collective-permute-start.4 = (bf16[128,1152]{1,0:T(8,128)(2,1)S(1)}, bf16[128,1152]{1,0:T(8,128)(2,1)S(1)}, u32[]{:S(2)}, u32[]{:S(2)}) collective-permute-start(bf16[128,1152]{1,0:T(8,128)(2,1)S(1)} %get-tuple-element.18), channel_id=1, source_target_pairs={{0,32},{16,48},{32,0},{48,16},{1,33},{17,49},{33,1},{49,17},{2,34}... | collective-permute-start | bytes 884744 | tf_op jit(solution)/shard_map/gather_sets/ppermute | solution.py:20
  24.6 15.9 %collective-permute-start.5 = (bf16[128,1152]{1,0:T(8,128)(2,1)S(1)}, bf16[128,1152]{1,0:T(8,128)(2,1)S(1)}, u32[]{:S(2)}, u32[]{:S(2)}) collective-permute-start(bf16[128,1152]{1,0:T(8,128)(2,1)S(1)} %get-tuple-element.18), channel_id=1, source_target_pairs={{0,48},{16,0},{32,16},{48,32},{1,49},{17,1},{33,17},{49,33},{2,50}... | collective-permute-start | bytes 884744 | tf_op jit(solution)/shard_map/gather_sets/ppermute | solution.py:20
  26.6 7.2 %collective-permute-start.8 = (bf16[144,512]{1,0:T(8,128)(2,1)S(1)}, bf16[144,512]{1,0:T(8,128)(2,1)S(1)}, u32[]{:S(2)}, u32[]{:S(2)}) collective-permute-start(bf16[144,512]{1,0:T(8,128)(2,1)S(1)} %pad_maximum_fusion.2), channel_id=1, source_target_pairs={{0,128},{128,1},{1,129},{129,0},{2,130},{130,3},{3,131},{131,2},{4... | collective-permute-start | bytes 442376 | tf_op jit(solution)/shard_map/gather_sets/ppermute | solution.py:27
  30.9 5.9 %collective-permute-start.10 = (bf16[144,512]{1,0:T(8,128)(2,1)S(1)}, bf16[144,512]{1,0:T(8,128)(2,1)S(1)}, u32[]{:S(2)}, u32[]{:S(2)}) collective-permute-start(bf16[144,512]{1,0:T(8,128)(2,1)S(1)} %pad_maximum_fusion.2), channel_id=1, source_target_pairs={{0,1},{128,129},{1,0},{129,128},{2,3},{130,131},{3,2},{131,130},{4... | collective-permute-start | bytes 442376 | tf_op jit(solution)/shard_map/gather_sets/ppermute | solution.py:27
  33.9 5.2 %collective-permute-start.12 = (bf16[144,512]{1,0:T(8,128)(2,1)S(1)}, bf16[144,512]{1,0:T(8,128)(2,1)S(1)}, u32[]{:S(2)}, u32[]{:S(2)}) collective-permute-start(bf16[144,512]{1,0:T(8,128)(2,1)S(1)} %pad_maximum_fusion.2), channel_id=1, source_target_pairs={{0,129},{128,0},{1,128},{129,1},{2,131},{130,2},{3,130},{131,3},{4... | collective-permute-start | bytes 442376 | tf_op jit(solution)/shard_map/gather_sets/ppermute | solution.py:27
  36.8 7.9 %collective-permute-start.9 = (bf16[144,512]{1,0:T(8,128)(2,1)S(1)}, bf16[144,512]{1,0:T(8,128)(2,1)S(1)}, u32[]{:S(2)}, u32[]{:S(2)}) collective-permute-start(bf16[144,512]{1,0:T(8,128)(2,1)S(1)} %collective-permute-done.8), channel_id=1, source_target_pairs={{0,2},{2,0},{1,3},{3,1},{4,6},{6,4},{5,7},{7,5},{8,10},{10,8},{9,1... | collective-permute-start | bytes 442376 | tf_op jit(solution)/shard_map/gather_sets/ppermute | solution.py:20
  39.1 5.7 %collective-permute-start.11 = (bf16[144,512]{1,0:T(8,128)(2,1)S(1)}, bf16[144,512]{1,0:T(8,128)(2,1)S(1)}, u32[]{:S(2)}, u32[]{:S(2)}) collective-permute-start(bf16[144,512]{1,0:T(8,128)(2,1)S(1)} %collective-permute-done.10), channel_id=1, source_target_pairs={{0,2},{2,0},{1,3},{3,1},{4,6},{6,4},{5,7},{7,5},{8,10},{10,8},{9,1... | collective-permute-start | bytes 442376 | tf_op jit(solution)/shard_map/gather_sets/ppermute | solution.py:20
  39.1 7.9 %collective-permute-start.13 = (bf16[144,512]{1,0:T(8,128)(2,1)S(1)}, bf16[144,512]{1,0:T(8,128)(2,1)S(1)}, u32[]{:S(2)}, u32[]{:S(2)}) collective-permute-start(bf16[144,512]{1,0:T(8,128)(2,1)S(1)} %collective-permute-done.12), channel_id=1, source_target_pairs={{0,2},{2,0},{1,3},{3,1},{4,6},{6,4},{5,7},{7,5},{8,10},{10,8},{9,1... | collective-permute-start | bytes 442376 | tf_op jit(solution)/shard_map/gather_sets/ppermute | solution.py:20
  40.7 7.4 %collective-permute-start.6 = (bf16[4,128,1152]{2,1,0:T(8,128)(2,1)S(1)}, bf16[4,128,1152]{2,1,0:T(8,128)(2,1)S(1)}, u32[]{:S(2)}, u32[]{:S(2)}) collective-permute-start(bf16[4,128,1152]{2,1,0:T(8,128)(2,1)S(1)} %pad_maximum_fusion), channel_id=1, source_target_pairs={{0,64},{64,0},{1,65},{65,1},{2,66},{66,2},{3,67},{67,3},{4,68},{68... | collective-permute-start | bytes 3538952 | tf_op jit(solution)/shard_map/gather_sets/ppermute | solution.py:20
  58.6 8.3 %collective-permute-start.14 = (f32[2,2,4,128]{3,2,1,0:T(4,128)S(1)}, f32[2,2,4,128]{3,2,1,0:T(4,128)S(1)}, u32[]{:S(2)}, u32[]{:S(2)}) collective-permute-start(f32[2,2,4,128]{3,2,1,0:T(4,128)S(1)} %pad_maximum_fusion.4), channel_id=1, source_target_pairs={{0,64},{64,0},{1,65},{65,1},{2,66},{66,2},{3,67},{67,3},{4,68},{68... | collective-permute-start | bytes 24584 | tf_op jit(solution)/shard_map/totals/ppermute | solution.py:20
  62.1 7.6 %collective-permute-start.20 = (f32[2,4,2,128]{3,2,1,0:T(2,128)S(1)}, f32[2,4,2,128]{3,2,1,0:T(2,128)S(1)}, u32[]{:S(2)}, u32[]{:S(2)}) collective-permute-start(f32[2,4,2,128]{3,2,1,0:T(2,128)S(1)} %maximum_add_fusion.2), channel_id=1, source_target_pairs={{0,1},{128,129},{1,0},{129,128},{2,3},{130,131},{3,2},{131,130},{4... | collective-permute-start | bytes 24584 | tf_op jit(solution)/shard_map/totals/ppermute | solution.py:27
  64.3 5.4 %collective-permute-start.19 = (f32[2,4,2,128]{3,2,1,0:T(2,128)S(1)}, f32[2,4,2,128]{3,2,1,0:T(2,128)S(1)}, u32[]{:S(2)}, u32[]{:S(2)}) collective-permute-start(f32[2,4,2,128]{3,2,1,0:T(2,128)S(1)} %maximum_add_fusion.2), channel_id=1, source_target_pairs={{0,128},{128,1},{1,129},{129,0},{2,130},{130,3},{3,131},{131,2},{4... | collective-permute-start | bytes 24584 | tf_op jit(solution)/shard_map/totals/ppermute | solution.py:27
  76.9 26.7 %collective-permute-start.22 = (f32[4,128,512]{2,1,0:T(8,128)}, f32[4,128,512]{2,1,0:T(8,128)}, u32[]{:S(2)}, u32[]{:S(2)}) collective-permute-start(f32[4,128,512]{2,1,0:T(8,128)} %fusion.68), channel_id=1, source_target_pairs={{0,64},{64,0},{1,65},{65,1},{2,66},{66,2},{3,67},{67,3},{4,68},{68... | collective-permute-start | bytes 3145736 | tf_op jit(solution)/shard_map/pull/ppermute | solution.py:20
  98.3 30.0 %all-to-all-start = ((bf16[64,8,512]{2,1,0:T(8,128)(2,1)}), bf16[64,8,512]{2,1,0:T(8,128)(2,1)S(1)}, u32[]{:S(2)}, u32[]{:S(2)}) async-start(bf16[64,8,512]{2,1,0:T(8,128)(2,1)} %fusion.14), calls=%async_computation | async-start | bytes 1048576 | tf_op jit(solution)/shard_map/head/all_to_all | solution.py:145
  105.2 7.5 %collective-permute-start.23 = (bf16[128,512]{1,0:T(8,128)(2,1)S(1)}, bf16[128,512]{1,0:T(8,128)(2,1)S(1)}, u32[]{:S(2)}, u32[]{:S(2)}) collective-permute-start(bf16[128,512]{1,0:T(8,128)(2,1)S(1)} %get-tuple-element.14), channel_id=1, source_target_pairs={{0,48},{16,0},{32,16},{48,32},{1,49},{17,1},{33,17},{49,33},{2,50}... | collective-permute-start | bytes 393224 | tf_op jit(solution)/shard_map/slopes/ppermute | solution.py:20
  107.7 8.4 %collective-permute-start.24 = (bf16[128,512]{1,0:T(8,128)(2,1)S(1)}, bf16[128,512]{1,0:T(8,128)(2,1)S(1)}, u32[]{:S(2)}, u32[]{:S(2)}) collective-permute-start(bf16[128,512]{1,0:T(8,128)(2,1)S(1)} %get-tuple-element.16), channel_id=1, source_target_pairs={{0,32},{16,48},{32,0},{48,16},{1,33},{17,49},{33,1},{49,17},{2,34}... | collective-permute-start | bytes 393224 | tf_op jit(solution)/shard_map/slopes/ppermute | solution.py:20
  108.1 13.6 %collective-permute-start.25 = (bf16[128,512]{1,0:T(8,128)(2,1)S(1)}, bf16[128,512]{1,0:T(8,128)(2,1)S(1)}, u32[]{:S(2)}, u32[]{:S(2)}) collective-permute-start(bf16[128,512]{1,0:T(8,128)(2,1)S(1)} %get-tuple-element.15), channel_id=1, source_target_pairs={{0,16},{16,32},{32,48},{48,0},{1,17},{17,33},{33,49},{49,1},{2,18}... | collective-permute-start | bytes 393224 | tf_op jit(solution)/shard_map/slopes/ppermute | solution.py:20
  122.0 7.2 %collective-permute-start.26 = (bf16[32,512]{1,0:T(8,128)(2,1)S(1)}, bf16[32,512]{1,0:T(8,128)(2,1)S(1)}, u32[]{:S(2)}, u32[]{:S(2)}) collective-permute-start(bf16[32,512]{1,0:T(8,128)(2,1)S(1)} %get-tuple-element.26), channel_id=1, source_target_pairs={{0,12},{4,0},{8,4},{12,8},{1,13},{5,1},{9,5},{13,9},{2,14},{6,2},{... | collective-permute-start | bytes 98312 | tf_op jit(solution)/shard_map/route_back/ppermute | solution.py:20
  124.9 6.8 %collective-permute-start.27 = (bf16[32,512]{1,0:T(8,128)(2,1)S(1)}, bf16[32,512]{1,0:T(8,128)(2,1)S(1)}, u32[]{:S(2)}, u32[]{:S(2)}) collective-permute-start(bf16[32,512]{1,0:T(8,128)(2,1)S(1)} %get-tuple-element.25), channel_id=1, source_target_pairs={{0,8},{4,12},{8,0},{12,4},{1,9},{5,13},{9,1},{13,5},{2,10},{6,14},... | collective-permute-start | bytes 98312 | tf_op jit(solution)/shard_map/route_back/ppermute | solution.py:20
  126.4 5.3 %collective-permute-start.28 = (bf16[32,512]{1,0:T(8,128)(2,1)S(1)}, bf16[32,512]{1,0:T(8,128)(2,1)S(1)}, u32[]{:S(2)}, u32[]{:S(2)}) collective-permute-start(bf16[32,512]{1,0:T(8,128)(2,1)S(1)} %get-tuple-element.24), channel_id=1, source_target_pairs={{0,4},{4,8},{8,12},{12,0},{1,5},{5,9},{9,13},{13,1},{2,6},{6,10},{... | collective-permute-start | bytes 98312 | tf_op jit(solution)/shard_map/route_back/ppermute | solution.py:20
  (16 other events, 86.9 us)
